TPU v7x, 256 devices: a whole 4x4x8 slice. The times are simulated.
256 devices in a mesh: dp: 8 (over x_hi, y), fsdp: 16 (over z, core), tensor: 2 (over x_lo).
Axes of the slice: x: 4 (x_hi: 2, x_lo: 2; x = x_hi * 2 + x_lo), y: 4, z: 8, core: 2. Of those that a mesh axis runs over, the one named last changes fastest.
Arguments:
- attn_out: bfloat16 [16384, 2560], P(('dp', 'fsdp')), may hold values from -6 to 6
- cotangent: bfloat16 [16384, 5120], P(('dp', 'fsdp'), 'tensor'), may hold values from -6 to 6
- old_weights: bfloat16 [3, 2048, 4096], P(None, 'tensor', 'fsdp'), may hold values from -0.125 to 0.125
- depth_coef: float32 [2], replicated, may hold values from 0.3 to 1
- depth_pick: int32 [2], replicated, may hold values from 0 to 2
- in_blocks: bfloat16 [20, 2, 128, 128], replicated, may hold values from -0.3125 to 0.3125
- in_cols: int32 [20, 2], replicated, may hold values from 0 to 15, all different within a row
- out_blocks: bfloat16 [40, 2, 128, 128], P('tensor'), may hold values from -0.375 to 0.375
- out_cols: int32 [40, 2], P('tensor'), may hold values from 0 to 31, all different within a row
Outputs:
- grown_out: bfloat16 [16384, 5120], P(('dp', 'fsdp'), 'tensor')
- grad_attn: bfloat16 [16384, 2560], P(('dp', 'fsdp'), 'tensor')
- grad_in_blocks: float32 [20, 2, 128, 128], P('tensor')
- grad_out_blocks: float32 [40, 2, 128, 128], P('tensor')
Inputs may be any that keep to these rules, and one draw needn't show every extreme that they name: `in_cols`: each row names 2 different old head blocks; every old head block is named by some row. `out_cols`: each row names 2 different old width blocks; every old width block is named by some row.
All inputs are finite; a program needn't handle non-finite values.
Results may differ from a plain program's by a relative error of at most 0.0095.
Values may be sent and summed in bfloat16 or wider, within the bound.
No kernel may reach another device: no remote copies, remote signals or barrier semaphores. Data moves between devices by JAX's collectives and lax.ppermute only.
A program may use at most 64 MiB of HBM per device.

v0:
```python
import jax
import jax.numpy as jnp
from jax import lax
from jax.sharding import PartitionSpec as P

HEAD = 128
D_OLD = 4096
HG_OLD = 16
HG_NEW = 20
DEPTH_K = 2
BO_OLD = 32


def gathered_mix(mixed_weight):
    return lax.all_gather(mixed_weight, "fsdp", axis=1, tiled=True)


def local(
    attn_out,
    cotangent,
    old_weights,
    depth_coef,
    depth_pick,
    in_blocks,
    in_cols,
    out_blocks,
    out_cols,
):
    highest = lax.Precision.HIGHEST
    tok_rows = attn_out.shape[0]
    tensor_half = lax.axis_index("tensor")
    tensor_count = lax.axis_size("tensor")
    local_old = old_weights.shape[1]
    local_blocks = local_old // HEAD
    rows_in = HG_NEW // tensor_count
    mixed_weight = jnp.zeros(old_weights.shape[1:], jnp.float32)
    for layer_slot in range(DEPTH_K):
        picked = lax.dynamic_index_in_dim(old_weights, depth_pick[layer_slot], 0, keepdims=False)
        mixed_weight = mixed_weight + depth_coef[layer_slot] * picked.astype(jnp.float32)
    mixed_weight = mixed_weight.astype(jnp.bfloat16)
    attn_blocks = attn_out.reshape(tok_rows, HG_NEW, HEAD)
    products = jnp.einsum(
        "trd,rkde->trke", attn_blocks, in_blocks, preferred_element_type=jnp.float32
    )
    local_cols = tensor_half * local_blocks + jnp.arange(local_blocks, dtype=jnp.int32)
    in_hot = (in_cols[:, :, None] == local_cols[None, None, :]).astype(jnp.float32)
    hidden_local = jnp.einsum("trke,rkc->tce", products, in_hot, precision=highest)
    hidden_local = hidden_local.reshape(tok_rows, local_old).astype(jnp.bfloat16)
    full_mix = gathered_mix(mixed_weight)
    old_part = jnp.dot(hidden_local, full_mix, preferred_element_type=jnp.float32)
    old_out = lax.psum(old_part.astype(jnp.bfloat16), "tensor")
    old_selected = jnp.take(old_out.reshape(tok_rows, BO_OLD, HEAD), out_cols, axis=1)
    grown_out = jnp.einsum(
        "trkd,rkde->tre", old_selected, out_blocks, preferred_element_type=jnp.float32
    )
    grown_out = grown_out.reshape(tok_rows, -1).astype(jnp.bfloat16)
    cot_blocks = cotangent.reshape(tok_rows, out_blocks.shape[0], HEAD)
    backward_terms = jnp.einsum(
        "tre,rkde->trkd", cot_blocks, out_blocks, preferred_element_type=jnp.float32
    )
    out_hot = (out_cols[:, :, None] == jnp.arange(BO_OLD, dtype=jnp.int32)[None, None, :]).astype(
        jnp.float32
    )
    grad_part = jnp.einsum("trkd,rkc->tcd", backward_terms, out_hot, precision=highest).reshape(
        tok_rows, D_OLD
    )
    old_grad = lax.psum(grad_part.astype(jnp.bfloat16), "tensor")
    hidden_grad_local = jnp.einsum(
        "to,fo->tf", old_grad, full_mix, preferred_element_type=jnp.float32
    ).astype(jnp.bfloat16)
    hidden_grad = lax.all_gather(hidden_grad_local, "tensor", axis=1, tiled=True)
    my_in_blocks = lax.dynamic_slice_in_dim(in_blocks, tensor_half * rows_in, rows_in, 0)
    my_in_cols = lax.dynamic_slice_in_dim(in_cols, tensor_half * rows_in, rows_in, 0)
    grad_selected = jnp.take(hidden_grad.reshape(tok_rows, HG_OLD, HEAD), my_in_cols, axis=1)
    grad_attn = jnp.einsum(
        "trke,rkde->trd", grad_selected, my_in_blocks, preferred_element_type=jnp.float32
    )
    grad_attn = grad_attn.reshape(tok_rows, rows_in * HEAD).astype(jnp.bfloat16)
    my_attn = lax.dynamic_slice_in_dim(attn_blocks, tensor_half * rows_in, rows_in, 1)
    in_terms = jnp.einsum(
        "trd,trke->rkde", my_attn, grad_selected, preferred_element_type=jnp.float32
    )
    out_terms = jnp.einsum(
        "trkd,tre->rkde", old_selected, cot_blocks, preferred_element_type=jnp.float32
    )
    in_sum, out_sum = lax.psum((in_terms, out_terms), ("dp", "fsdp"))
    grad_scale = float(tok_rows * lax.axis_size("dp") * lax.axis_size("fsdp")) ** (-0.5)
    return (grown_out, grad_attn, in_sum * grad_scale, out_sum * grad_scale)


def solution(mesh):
    placed = (
        P(("dp", "fsdp"), None),
        P(("dp", "fsdp"), "tensor"),
        P(None, "tensor", "fsdp"),
        P(),
        P(),
        P(),
        P(),
        P("tensor", None, None, None),
        P("tensor", None),
    )
    return jax.shard_map(
        local,
        mesh=mesh,
        in_specs=placed,
        out_specs=(
            P(("dp", "fsdp"), "tensor"),
            P(("dp", "fsdp"), "tensor"),
            P("tensor", None, None, None),
            P("tensor", None, None, None),
        ),
        check_vma=False,
    )
```

profile of v0, /device:TPU:6, one launch (start us, length us, event | category | flops | bytes accessed | tf_op | source)
XLA Modules:
  0.0 1481.5 jit_solution(9573268355496351866)
XLA Ops:
  7.2 0.0 copy-start
  7.2 0.0 all-gather.3.cloned.1.call-start
  7.2 1.3 fusion.55
  11.2 1.3 fusion.54
  13.8 3.5 add_convert_fusion
  17.3 0.0 all-gather.3.cloned.1.call-update
  17.4 0.0 all-reduce.7.cloned.1.call-start
  17.4 1.5 copy.27
  18.9 2.0 fusion.56
  21.0 3.6 copy.45
  24.6 0.3 copy.34
  24.9 2.0 fusion.57
  26.9 3.6 copy.51
  30.5 3.5 bitcast_convert_fusion
  34.0 1.4 copy.71
  35.5 3.0 fusion.24
  38.5 46.0 %all-gather.3.cloned.1.call-done = bf16[1,1024,4096]{2,1,0:T(8,128)(2,1)} async-done(((bf16[1,1024,256]{2,1,0:T(8,128)(2,1)}), bf16[1,1024,4096]{2,1,0:T(8,128)(2,1)}) %all-gather.3.cloned.1.call-update) | async-done | bytes 8388624 | tf_op jit(solution)/shard_map/all_gather | solution.py:15
  84.5 4.7 fusion.13
  89.1 1.3 copy.72
  90.4 0.0 all-reduce.7.cloned.1.call-update
  90.4 0.0 all-reduce.5.cloned.1.call-start
  90.5 0.1 compare_and_fusion
  90.6 0.1 copy.35
  90.7 0.1 reshape.66
  90.7 0.1 copy.33
  90.8 0.1 copy.29
  91.0 0.1 reshape.58
  91.1 0.1 copy.26
  91.2 72.4 %all-reduce.7.cloned.1.call-done = (bf16[128,32,128]{2,0,1:T(8,128)(2,1)}, bf16[128,4096]{1,0:T(8,128)(2,1)}) async-done(((bf16[128,32,128]{2,0,1:T(8,128)(2,1)}, bf16[128,4096]{1,0:T(8,128)(2,1)}), (bf16[128,32,128]{2,0,1:T(8,128)(2,1)}, bf16[128,4096]{1,0:T(8,128)(2,1)})) %all-reduce.7.cloned.1.call-update) | async-done | bytes 2097168 | tf_op jit(solution)/shard_map/psum | solution.py:51
  163.5 6.6 fusion.27
  170.2 8.7 all_gather.7
  178.9 0.1 copy_bitcast_fusion.2
  179.0 0.7 gather_fusion.1
  179.7 1.1 copy.37
  180.8 3.1 gather_fusion
  183.9 1.8 copy.30
  185.7 2.0 fusion.17
  187.7 1.4 convolution_bitcast_fusion
  189.1 0.0 all-reduce.5.cloned.1.call-update
  189.2 1.1 copy-done.4
  190.2 2.2 fusion.23
  192.4 1.9 copy.42
  194.3 0.6 fusion.16
  194.9 1.1 copy.41
  196.0 1273.8 %all-reduce.5.cloned.1.call-done = (f32[10,2,128,128]{2,3,1,0:T(8,128)}, f32[20,2,128,128]{3,2,1,0:T(8,128)}) async-done(((f32[10,2,128,128]{2,3,1,0:T(8,128)}, f32[20,2,128,128]{3,2,1,0:T(8,128)}), (f32[10,2,128,128]{2,3,1,0:T(8,128)}, f32[20,2,128,128]{3,2,1,0:T(8,128)})) %all-reduce.5.cloned.1.call-update) | async-done | bytes 3932176 | tf_op jit(solution)/shard_map/psum | solution.py:86
  1469.8 3.6 broadcast_multiply_fusion
  1473.4 0.1 broadcast_multiply_fusion.1
  1473.5 1.5 copy.43
  (23 shorter events, 0.1 us)
Async XLA Ops:
  7.2 17.8 %copy-start = (bf16[20,2,128,128]{3,2,1,0:T(8,128)(2,1)S(1)}, bf16[20,2,128,128]{3,2,1,0:T(8,128)(2,1)}, u32[]{:S(2)}) copy-start(bf16[20,2,128,128]{3,2,1,0:T(8,128)(2,1)} %param.16) | copy-start | bytes 3932164
  7.2 77.3 %all-gather.3.cloned.1.call-start = ((), (), s32[]{:S(2)}) async-start(), calls=%async_computation | async-start | bytes 8912896 | tf_op jit(solution)/shard_map/all_gather | solution.py:15
  17.3 1.6 copy-start.6
  17.4 146.2 %all-reduce.7.cloned.1.call-start = ((), (), s32[]{:S(2)}) async-start(), calls=%async_computation.2 | async-start | bytes 4194304 | tf_op jit(solution)/shard_map/psum | solution.py:51
  18.9 2.1 copy-start.1
  21.0 3.6 copy-start.7
  26.9 3.6 copy-start.9
  34.0 1.4 copy-start.8
  90.4 1379.4 %all-reduce.5.cloned.1.call-start = ((), (), s32[]{:S(2)}) async-start(), calls=%async_computation.1 | async-start | bytes 7864320 | tf_op jit(solution)/shard_map/psum | solution.py:86
  185.6 2.1 copy-start.2
  185.6 2.1 copy-start.3
  189.1 1.1 copy-start.4
  1469.8 3.6 copy-start.5
Sparse Core Ops, SparseCore 0:
  17.5 66.9 all-gather.2
  90.5 72.9 all-reduce.6
  189.3 1280.4 all-reduce.4
where the time goes:
time: 1480 us
  waiting for transfers between devices  1390 us (94%)
  matrix products  28.2 us (2%)
  local copies, waits for them, and re-layouts  27.2 us (2%)
  between operations  17.8 us (1%)
    psum x1, waiting for transfers between devices, local(): in_sum, out_sum = lax.psum((in_terms, out_terms), ('dp', 'fsdp'))  1270 us
    psum x1, waiting for transfers between devices, local(): old_out = lax.psum(old_part.astype(jnp.bfloat16), 'tensor')  72.4 us
    all_gather x1, waiting for transfers between devices, gathered_mix(): return lax.all_gather(mixed_weight, 'fsdp', axis=1, tiled=True)  46 us
  transfers between devices with their start and end apart: 3, of which 3 were waited for; matrix products, arithmetic and copies ran while one was open for 2% of the time, Pallas kernels for 0%

commit v1 on v0

--- a/solution.py
+++ b/solution.py
@@ -83,7 +83,7 @@
     out_terms = jnp.einsum(
         "trkd,tre->rkde", old_selected, cot_blocks, preferred_element_type=jnp.float32
     )
-    in_sum, out_sum = lax.psum((in_terms, out_terms), ("dp", "fsdp"))
+    in_sum, out_sum = lax.psum(lax.psum((in_terms, out_terms), "fsdp"), "dp")
     grad_scale = float(tok_rows * lax.axis_size("dp") * lax.axis_size("fsdp")) ** (-0.5)
     return (grown_out, grad_attn, in_sum * grad_scale, out_sum * grad_scale)
 

time: 1480 us -> 439 us (0.30)
  waiting for transfers between devices: 1390 us -> 347 us
    psum x1 -> x2, waiting for transfers between devices: 1270 us -> 229 us  [local(): in_sum, out_sum = lax.psum(lax.psum((in_terms, out_terms), 'fsdp'), 'dp')]
  transfers between devices with their start and end apart: 3 -> 4, of which waited for: 3 -> 4; matrix products, arithmetic and copies ran while one was open for 2% -> 6% of each run, Pallas kernels for 0% -> 0%
where the time goes in v1:
time: 439 us; the launch traced here: 437 us
  waiting for transfers between devices  347 us (79%)
  matrix products  28.2 us (6%)
  local copies, waits for them, and re-layouts  27.1 us (6%)
  between operations  17.8 us (4%)
  blocking collectives  8.54 us (2%)
  other arithmetic  7.38 us (2%)
    psum x2, waiting for transfers between devices, local(): in_sum, out_sum = lax.psum(lax.psum((in_terms, out_terms), 'fsdp'), 'dp')  229 us
    psum x1, waiting for transfers between devices, local(): old_out = lax.psum(old_part.astype(jnp.bfloat16), 'tensor')  72.7 us
    all_gather x1, waiting for transfers between devices, gathered_mix(): return lax.all_gather(mixed_weight, 'fsdp', axis=1, tiled=True)  46 us
  transfers between devices with their start and end apart: 4, of which 4 were waited for; matrix products, arithmetic and copies ran while one was open for 6% of the time, Pallas kernels for 0%

profile of v1, /device:TPU:6, one launch (start us, length us, event | category | flops | bytes accessed | tf_op | source)
XLA Modules:
  0.0 436.5 jit_solution(8258386780648789214)
XLA Ops:
  7.2 0.0 all-gather.3.cloned.1.call-start
  7.2 1.3 fusion.55
  11.2 1.3 fusion.54
  13.8 3.5 add_convert_fusion
  17.3 0.0 all-gather.3.cloned.1.call-update
  17.4 0.0 all-reduce.11.cloned.1.call-start
  17.4 1.5 copy.27
  18.9 2.0 fusion.56
  21.0 3.6 copy.45
  24.6 0.3 copy.34
  24.9 2.0 fusion.57
  26.9 3.6 copy.51
  30.4 3.5 bitcast_convert_fusion
  34.0 1.4 copy.71
  35.4 3.0 fusion.24
  38.4 46.0 %all-gather.3.cloned.1.call-done = bf16[1,1024,4096]{2,1,0:T(8,128)(2,1)} async-done(((bf16[1,1024,256]{2,1,0:T(8,128)(2,1)}), bf16[1,1024,4096]{2,1,0:T(8,128)(2,1)}) %all-gather.3.cloned.1.call-update) | async-done | bytes 8388624 | tf_op jit(solution)/shard_map/all_gather | solution.py:15
  84.4 4.7 %fusion.13 = bf16[16,32,8,128]{3,2,1,0:T(8,128)(2,1)S(1)} fusion(bf16[1,1024,4096]{2,1,0:T(8,128)(2,1)} %all-gather.3.cloned.1.call-done, bf16[16,8,8,128]{3,2,1,0:T(8,128)(2,1)S(1)} %bitcast.126), kind=kOutput, calls=%fused_computation.14 | convolution fusion | flops 1074266112 | bytes 9699328 | tf_op jit(solution)/shard_map/dot_general | solution.py:50
  89.1 1.3 copy.72
  90.4 0.0 all-reduce.11.cloned.1.call-update
  90.4 0.0 all-reduce.7.cloned.1.call-start
  90.4 0.1 compare_and_fusion
  90.5 0.1 copy.35
  90.6 0.1 reshape.66
  90.7 0.1 copy.33
  90.8 0.1 copy.29
  90.9 0.1 reshape.58
  91.0 0.1 copy.26
  91.2 72.7 %all-reduce.11.cloned.1.call-done = (bf16[128,32,128]{2,0,1:T(8,128)(2,1)}, bf16[128,4096]{1,0:T(8,128)(2,1)}) async-done(((bf16[128,32,128]{2,0,1:T(8,128)(2,1)}, bf16[128,4096]{1,0:T(8,128)(2,1)}), (bf16[128,32,128]{2,0,1:T(8,128)(2,1)}, bf16[128,4096]{1,0:T(8,128)(2,1)})) %all-reduce.11.cloned.1.call-update) | async-done | bytes 2097168 | tf_op jit(solution)/shard_map/psum | solution.py:51
  163.9 6.6 %fusion.27 = bf16[128,1024]{1,0:T(8,128)(2,1)S(1)} fusion(bf16[128,4096]{1,0:T(8,128)(2,1)} %get-tuple-element.17, bf16[1,1024,4096]{2,1,0:T(8,128)(2,1)} %all-gather.3.cloned.1.call-done), kind=kOutput, calls=%fused_computation.25 | convolution fusion | flops 1073872896 | bytes 9699328 | tf_op jit(solution)/shard_map/to,fo->tf/dot_general | solution.py:68
  170.5 8.5 %all_gather.7 = bf16[128,2048]{1,0:T(8,128)(2,1)S(1)} all-gather(bf16[128,1024]{1,0:T(8,128)(2,1)S(1)} %fusion.27), channel_id=1, replica_groups=mesh['dp'=8,'fsdp'=16,'tensor'=2] {'tensor'}, dimensions={1}, use_global_device_ids=true | all-gather | bytes 786432 | tf_op jit(solution)/shard_map/all_gather | solution.py:71
  179.1 0.1 copy_bitcast_fusion.2
  179.2 0.7 gather_fusion.1
  179.9 1.1 copy.37
  181.0 3.1 gather_fusion
  184.0 1.8 copy.30
  185.8 2.0 fusion.17
  187.9 1.4 convolution_bitcast_fusion
  189.3 0.0 all-reduce.9.cloned.1.call-start
  189.4 122.8 %all-reduce.7.cloned.1.call-done = (f32[10,2,128,128]{2,3,1,0:T(8,128)}, f32[20,2,128,128]{3,2,1,0:T(8,128)}) async-done(((f32[10,2,128,128]{2,3,1,0:T(8,128)}, f32[20,2,128,128]{3,2,1,0:T(8,128)}), (f32[10,2,128,128]{2,3,1,0:T(8,128)}, f32[20,2,128,128]{3,2,1,0:T(8,128)})) %all-reduce.7.cloned.1.call-update) | async-done | bytes 3932176 | tf_op jit(solution)/shard_map/psum | solution.py:86
  312.2 1.1 copy-done.4
  313.3 2.2 fusion.23
  315.5 1.9 copy.42
  317.3 0.6 fusion.16
  318.0 1.1 copy.41
  319.1 105.7 %all-reduce.9.cloned.1.call-done = (f32[10,2,128,128]{2,3,1,0:T(8,128)}, f32[20,2,128,128]{3,2,1,0:T(8,128)}) async-done(((f32[10,2,128,128]{2,3,1,0:T(8,128)}, f32[20,2,128,128]{3,2,1,0:T(8,128)}), (f32[10,2,128,128]{2,3,1,0:T(8,128)}, f32[20,2,128,128]{3,2,1,0:T(8,128)})) %all-reduce.9.cloned.1.call-update) | async-done | bytes 3932176 | tf_op jit(solution)/shard_map/psum | solution.py:86
  424.8 3.6 broadcast_multiply_fusion
  428.4 0.1 broadcast_multiply_fusion.1
  428.5 1.5 copy.43
  (26 shorter events, 0.1 us)
Async XLA Ops:
  7.2 17.7 %copy-start = (bf16[20,2,128,128]{3,2,1,0:T(8,128)(2,1)S(1)}, bf16[20,2,128,128]{3,2,1,0:T(8,128)(2,1)}, u32[]{:S(2)}) copy-start(bf16[20,2,128,128]{3,2,1,0:T(8,128)(2,1)} %param.16) | copy-start | bytes 3932164
  7.2 77.2 %all-gather.3.cloned.1.call-start = ((), (), s32[]{:S(2)}) async-start(), calls=%async_computation | async-start | bytes 8912896 | tf_op jit(solution)/shard_map/all_gather | solution.py:15
  17.3 1.6 copy-start.6
  17.4 146.5 %all-reduce.11.cloned.1.call-start = ((), (), s32[]{:S(2)}) async-start(), calls=%async_computation.3 | async-start | bytes 4194304 | tf_op jit(solution)/shard_map/psum | solution.py:51
  18.9 2.1 copy-start.1
  21.0 3.6 copy-start.7
  26.9 3.6 copy-start.9
  34.0 1.4 copy-start.8
  90.4 221.8 %all-reduce.7.cloned.1.call-start = ((), (), s32[]{:S(2)}) async-start(), calls=%async_computation.1 | async-start | bytes 7864320 | tf_op jit(solution)/shard_map/psum | solution.py:86
  185.8 2.1 copy-start.2
  185.8 2.1 copy-start.3
  189.3 235.5 %all-reduce.9.cloned.1.call-start = ((), (), s32[]{:S(2)}) async-start(), calls=%async_computation.2 | async-start | bytes 7864320 | tf_op jit(solution)/shard_map/psum | solution.py:86
  312.2 1.1 copy-start.4
  424.8 3.6 copy-start.5
Sparse Core Ops, SparseCore 0:
  17.5 66.9 all-gather.2
  90.5 73.3 all-reduce.10
  189.5 122.6 all-reduce.6
  314.8 109.9 all-reduce.8
